TPU v7x, 32 devices: a whole 2x2x4 slice. The times are simulated.
32 devices in a mesh: beam: 2 (over y), freq: 8 (over z, x), tm: 2 (over core).
Axes of the slice: x: 2, y: 2, z: 4, core: 2. Of those that a mesh axis runs over, the one named last changes fastest.
Arguments:
- spectra: float32 [256, 16384], P(('beam', 'freq'), 'tm'), parts along dimension 0, may hold values from -250 to 250
- local_delays: int32 [4, 3, 128], P(None, None, 'freq'), may hold values from 0 to 8, as said below
- merge_delays: int32 [3, 3, 128], P(None, None, 'freq'), may hold values from 0 to 64, as said below
- widths: int32 [16], replicated, may hold values from 1 to 32, as said below
Outputs:
- detections: float32 [256, 16384], P(('beam', 'freq'), 'tm'), parts along dimension 0
There are 2 independent parts, one for each index of `beam`. A program takes and returns all parts, laid end to end along the dimension named above; an argument that names none is the same for every part. Nothing has to cross between parts.
Inputs may be any that keep to these rules, and one draw needn't show every extreme that they name: `local_delays`: entries [s, 0, r] and [s, 1, r] lie in 0 to 2**s - 1, entry [s, 2, r] in 0 to 2**s, and [s, 2, 0] equals 2**s. `merge_delays`: entries [j, 0, r] and [j, 1, r] lie in 0 to 15, entry [j, 2, r] in 0 to 16 * 2**j, and [j, 2, 0] equals 16 * 2**j. 16 distinct widths, one of them 32.
All inputs are finite; a program needn't handle non-finite values.
Results may differ from a plain program's by a relative error of at most 0.00002.
Values sent between devices are 32-bit elements; how exact they have to be, the bound alone decides.
A program may use at most 64 MiB of HBM per device.

v0:
```python
import functools
import math

import jax
import jax.numpy as jnp
from jax import lax
from jax.experimental import pallas as pl
from jax.experimental.pallas import tpu as pltpu
from jax.sharding import PartitionSpec as P

WMAX = 32
EPSILON = 1e-05
LANES = 128
SUB = 8
MESH = pl.DeviceIdType.MESH
FIRST_LAG = 1
MID_LAG = 1
LAST_LAG = 3
UNROLL = 16


def kernel(geo, x_ref, ld_ref, md_ref, w_ref, o_ref, *scratch):
    channels, chunks, freq_count, halo_chunks, tile = geo
    groups = channels // SUB
    llevels = channels.bit_length() - 1
    flevels = freq_count.bit_length() - 1
    samples = chunks * LANES
    nwidth = w_ref.shape[0]
    halo, st_own, st_peer, nrm, fin, eb, tri, scl = scratch[:8]
    loc = scratch[8 : 8 + llevels]
    count = chunks // tile
    flat_bufs = scratch[8 + llevels : 8 + llevels + flevels * count]
    bufs = [flat_bufs[j * count : (j + 1) * count] for j in range(flevels)]
    hsend, hrecv, ssend, srecv, bsend, brecv = scratch[8 + llevels + flevels * count :]

    tm = lax.axis_index("tm")
    freq = lax.axis_index("freq")
    peer = {"tm": 1 - tm}
    sides, partners = [], []
    for j in range(flevels):
        stride = 2**j
        side = (freq // stride) % 2
        sides.append(side)
        partners.append({"freq": freq + stride - 2 * stride * side})

    barrier = pltpu.get_barrier_semaphore()
    for other in [peer] + partners:
        pl.semaphore_signal(barrier, inc=1, device_id=other, device_id_type=MESH)

    lane = lax.broadcasted_iota(jnp.int32, (SUB, LANES), 1)

    for g in range(groups):
        block = x_ref[pl.ds(g * chunks * SUB, chunks * SUB), :].reshape(chunks, SUB, LANES)
        mean = jnp.sum(jnp.sum(block, axis=0), axis=1, keepdims=True) / samples
        off = block - mean[None]
        square = jnp.sum(jnp.sum(off * off, axis=0), axis=1, keepdims=True)
        st_own[0, pl.ds(g * SUB, SUB), :] = jnp.broadcast_to(mean, (SUB, LANES))
        st_own[1, pl.ds(g * SUB, SUB), :] = jnp.broadcast_to(square, (SUB, LANES))

    pl.semaphore_wait(barrier, 1 + flevels)
    stat_copy = pltpu.make_async_remote_copy(
        src_ref=st_own, dst_ref=st_peer, send_sem=ssend, recv_sem=srecv,
        device_id=peer, device_id_type=MESH,
    )
    stat_copy.start()
    halo_copies = []
    for g in range(groups):
        copy = pltpu.make_async_remote_copy(
            src_ref=x_ref.at[pl.ds(g * chunks * SUB, halo_chunks * SUB), :],
            dst_ref=halo.at[g],
            send_sem=hsend.at[g], recv_sem=hrecv.at[g],
            device_id=peer, device_id_type=MESH,
        )
        copy.start()
        halo_copies.append(copy)

    before = lax.broadcasted_iota(jnp.int32, (LANES, 2 * LANES), 0)
    after = lax.broadcasted_iota(jnp.int32, (LANES, 2 * LANES), 1)
    tri[...] = jnp.where(before < after, 1.0, 0.0)
    norm = 1.0 / math.sqrt(channels * freq_count)
    for i in range(nwidth):
        wide = jnp.full((SUB, LANES), w_ref[i].astype(jnp.float32), jnp.float32)
        scl[i] = (1.0 / jnp.sqrt(wide)) * norm

    stat_copy.wait_recv()
    mean_a, mean_b = st_own[0], st_peer[0]
    gap = mean_a - mean_b
    variance = (st_own[1] + st_peer[1] + gap * gap * (samples / 2)) / (2 * samples)
    nrm[0] = (mean_a + mean_b) * 0.5
    nrm[1] = 1.0 / jnp.sqrt(variance + EPSILON)
    for copy in halo_copies:
        copy.wait_recv()

    keep = jnp.where(tm == 0, 1.0, 0.0)

    def rows(body):
        for g in range(groups):
            body(g)

    def normalise(c0, size, is_halo):
        def body(g):
            out = []
            for i in range(SUB):
                r = g * SUB + i
                if is_halo:
                    part = halo[g, pl.ds(i, halo_chunks, stride=SUB), :]
                    gain = nrm[1, pl.ds(r, 1), :] * keep
                else:
                    part = x_ref[pl.ds(g * chunks * SUB + c0 * SUB + i, size, stride=SUB), :]
                    gain = nrm[1, pl.ds(r, 1), :]
                out.append((part - nrm[0, pl.ds(r, 1), :]) * gain)
            for i in range(SUB):
                r = g * SUB + i
                count = halo_chunks if is_halo else size
                loc[0][r, pl.ds(c0, count), :] = out[i]

        rows(body)

    def merged(low, high, lag, span, c0, size):
        if span < LANES:
            jump = 0
        else:
            jump = lag // LANES
            lag = lag % LANES
        cur = high(c0 + jump, size)
        nxt = high(c0 + jump + 1, size)
        lanes = lax.broadcasted_iota(jnp.int32, (size, LANES), 1)
        mixed = jnp.where(lanes < lag, nxt, cur)
        return low(c0, size) + pltpu.roll(mixed, (LANES - lag) % LANES, 1)

    def put(level, k, r, rel, size, value):
        bufs[level][k][sides[level], r, pl.ds(rel, size), :] = value

    def local_level(s, k, c0, size):
        span = 2**s
        src = loc[s]

        def body(g):
            out = []
            for i in range(SUB):
                r = g * SUB + i
                base = (r // (2 * span)) * (2 * span)
                lo_row = base + ld_ref[0, s, r]
                hi_row = base + span + ld_ref[1, s, r]
                out.append(merged(
                    lambda c, n: src[lo_row, pl.ds(c, n), :],
                    lambda c, n: src[hi_row, pl.ds(c, n), :],
                    ld_ref[2, s, r], span, c0, size,
                ))
            for i in range(SUB):
                r = g * SUB + i
                if s + 1 < llevels:
                    loc[s + 1][r, pl.ds(c0, size), :] = out[i]
                else:
                    put(0, k, r, c0 - pieces[k][0], size, out[i])

        rows(body)

    def merge_level(j, k, c0, size):
        span = channels * 2**j
        src = bufs[j][k]

        def body(g):
            out = []
            for i in range(SUB):
                r = g * SUB + i
                lo_row = md_ref[j, 0, r]
                hi_row = md_ref[j, 1, r]
                out.append(merged(
                    lambda c, n: src[0, lo_row, pl.ds(c, n), :],
                    lambda c, n: src[1, hi_row, pl.ds(c, n), :],
                    md_ref[j, 2, r], span, c0, size,
                ))
            for i in range(SUB):
                r = g * SUB + i
                if j + 1 < flevels:
                    put(j + 1, k, r, c0, size, out[i])
                else:
                    fin[pl.ds(pl.multiple_of(r * SUB, SUB), SUB), :] = out[i]

        rows(body)

    def prefix(c0):
        sums = jnp.dot(
            fin[...], tri[...], precision=lax.Precision.HIGHEST,
            preferred_element_type=jnp.float32,
        )
        own = sums[:, :LANES].reshape(channels, SUB, LANES)
        eb[:, pl.ds(c0, SUB), :] = own
        return own, sums[:, LANES:].reshape(channels, SUB, LANES)

    def boxcar(c0):
        own, total = prefix(c0)
        far = total + eb[:, pl.ds(c0 + 1, SUB), :]
        lanes = lax.broadcasted_iota(jnp.int32, (channels, SUB, LANES), 2)

        def body(at, best):
            for u in range(unroll):
                i = at * unroll + u
                wide = w_ref[i]
                mixed = jnp.where(lanes < wide, far, own)
                ahead = pltpu.roll(mixed, LANES - wide, 2)
                best = jnp.maximum(best, (ahead - own) * scl[i][None])
            return best

        unroll = math.gcd(nwidth, UNROLL)
        best = lax.fori_loop(
            0, nwidth // unroll, body, jnp.full((channels, SUB, LANES), -jnp.inf, jnp.float32)
        )
        for r in range(channels):
            at = (r // SUB) * chunks * SUB + c0 * SUB + r % SUB
            o_ref[pl.ds(at, SUB, stride=SUB), :] = best[r]

    halo_size = -(-halo_chunks // SUB) * SUB
    pieces = [(chunks - tile * (k + 1), tile) for k in range(count)]

    def tiles(k):
        found = [(pieces[k][0], tile, False)]
        if k == 0:
            found.insert(0, (chunks, halo_size, True))
        return found

    copies = {}
    for j in range(flevels):
        for k in range(count):
            size = tile
            if k == 0:
                size = size + halo_chunks
            window = bufs[j][k].at[sides[j], :, pl.ds(0, size), :]
            copies[j, k] = pltpu.make_async_remote_copy(
                src_ref=window, dst_ref=window,
                send_sem=bsend.at[j, k], recv_sem=brecv.at[j, k],
                device_id=partners[j], device_id_type=MESH,
            )

    def local_stage(k):
        for c0, size, is_halo in tiles(k):
            normalise(c0, size, is_halo)
            for s in range(llevels):
                local_level(s, k, c0, size)
        copies[0, k].start()

    def merge_stage(j, k):
        copies[j, k].wait_recv()
        if k:
            over = channels * 2**j // LANES + 1
            bufs[j][k][:, :, pl.ds(tile, over), :] = bufs[j][k - 1][:, :, pl.ds(0, over), :]
        for c0, size, is_halo in tiles(k):
            rel = c0 - pieces[k][0]
            if j + 1 < flevels:
                merge_level(j, k, rel, size)
            elif is_halo:
                merge_level(j, k, rel, SUB)
                prefix(c0)
            else:
                for sub in reversed(range(size // SUB)):
                    merge_level(j, k, rel + sub * SUB, SUB)
                    boxcar(c0 + sub * SUB)
        if j + 1 < flevels:
            copies[j + 1, k].start()

    lags = [FIRST_LAG] + [MID_LAG] * (flevels - 2) + [LAST_LAG]
    behind = [sum(lags[: j + 1]) for j in range(flevels)]
    for step in range(count + behind[-1]):
        if step < count:
            local_stage(step)
        for j in range(flevels):
            if 0 <= step - behind[j] < count:
                merge_stage(j, step - behind[j])

    stat_copy.wait_send()
    for copy in halo_copies:
        copy.wait_send()
    for copy in copies.values():
        copy.wait_send()


def per_device(mesh_shape, spectra, local_delays, merge_delays, widths):
    channels, block_len = spectra.shape
    freq_count = mesh_shape["freq"]
    chunks = block_len // LANES
    groups = channels // SUB
    tile = SUB
    halo_chunks = -(-(channels * freq_count - 1 + LANES) // LANES)
    halo_size = -(-halo_chunks // SUB) * SUB
    over = -(-(channels * freq_count // 2 // LANES + 1) // SUB) * SUB
    depth = chunks + halo_size + SUB
    llevels = channels.bit_length() - 1
    flevels = freq_count.bit_length() - 1
    count = chunks // tile
    f32 = jnp.float32
    flat = spectra.reshape(groups, SUB, chunks, LANES).transpose(0, 2, 1, 3)
    flat = flat.reshape(groups * chunks * SUB, LANES)
    smem = pl.BlockSpec(memory_space=pltpu.SMEM)
    vmem = pl.BlockSpec(memory_space=pltpu.VMEM)
    dma = pltpu.SemaphoreType.DMA
    out = pl.pallas_call(
        functools.partial(kernel, (channels, chunks, freq_count, halo_chunks, tile)),
        out_shape=pltpu.VMEM(flat.shape, f32),
        in_specs=[vmem, smem, smem, smem],
        out_specs=vmem,
        scratch_shapes=[
            pltpu.VMEM((groups, halo_chunks * SUB, LANES), f32),
            pltpu.VMEM((2, channels, LANES), f32),
            pltpu.VMEM((2, channels, LANES), f32),
            pltpu.VMEM((2, channels, LANES), f32),
            pltpu.VMEM((channels * SUB, LANES), f32),
            pltpu.VMEM((channels, depth, LANES), f32),
            pltpu.VMEM((LANES, 2 * LANES), f32),
            pltpu.VMEM((widths.shape[0], SUB, LANES), f32),
        ]
        + [pltpu.VMEM((channels, depth, LANES), f32)] * llevels
        + ([pltpu.VMEM((2, channels, tile + halo_size + over, LANES), f32)]
           + [pltpu.VMEM((2, channels, tile + over, LANES), f32)] * (count - 1)) * flevels
        + [
            dma((groups,)), dma((groups,)), dma, dma,
            dma((flevels, count)), dma((flevels, count)),
        ],
        compiler_params=pltpu.CompilerParams(
            collective_id=0, has_side_effects=True, vmem_limit_bytes=56 * 2**20
        ),
    )(flat, local_delays.transpose(1, 0, 2), merge_delays, widths)
    out = out.reshape(groups, chunks, SUB, LANES).transpose(0, 2, 1, 3)
    return out.reshape(channels, block_len)


def solution(mesh):
    placed = (P(("beam", "freq"), "tm"), P(None, None, "freq"), P(None, None, "freq"), P())
    return jax.shard_map(
        functools.partial(per_device, dict(mesh.shape)), mesh=mesh, in_specs=placed,
        out_specs=P(("beam", "freq"), "tm"), check_vma=False,
    )
```

profile of v0, /device:TPU:0, one launch (start us, length us, event | category | flops | bytes accessed | tf_op | source)
XLA Modules:
  0.0 42.2 jit_solution(13077965989395054019)
XLA Ops:
  0.0 41.4 %shard_map.46 = f32[1024,128]{1,0:T(8,128)S(1)} custom-call(f32[1024,128]{1,0:T(8,128)} %bitcast.12, s32[3,4,16]{2,1,0:T(4,128)} %bitcast.13, s32[3,3,16]{2,1,0:T(4,128)} %md_ref.1, s32[16]{0:T(128)} %w_ref.1), custom_call_target="tpu_custom_call" | custom-call | tf_op jit(solution)/shard_map/pallas_call | solution.py:297
  41.4 0.8 %copy.6 = f32[16,8192]{1,0:T(8,128)} copy(f32[16,8192]{1,0:T(8,128)S(1)} %bitcast.11) | data formatting | bytes 1048576
where the time goes:
time: 42.3 us; the launch traced here: 42.2 us
  Pallas kernels  41.4 us (98%)
  local copies, waits for them, and re-layouts  0.8 us (2%)
    pallas_call x1, Pallas kernels, per_device(): pl.pallas_call(functools.partial(kernel, (channels, chunks, freq_count, h...  41.4 us

commit v1 on v0

v1 whole, which is shorter than its diff:
```python
import functools
import math

import jax
import jax.numpy as jnp
from jax import lax
from jax.experimental import pallas as pl
from jax.experimental.pallas import tpu as pltpu
from jax.sharding import PartitionSpec as P

WMAX = 32
EPSILON = 1e-05
LANES = 128
SUB = 8
MESH = pl.DeviceIdType.MESH
FIRST_LAG = 1
MID_LAG = 1
LAST_LAG = 3
UNROLL = 16
MAX_SPLIT = 2


def flip(value, mask):
    bit = 1
    while bit <= mask:
        if mask & bit:
            value = value + bit - 2 * bit * ((value // bit) % 2)
        bit *= 2
    return value


def kernel(geo, names, x_ref, ld_ref, md_ref, w_ref, o_ref, *scratch):
    channels, chunks, freq_count, halo_chunks, split = geo
    ref = dict(zip(names, scratch))
    sets = 2**split
    groups = channels // SUB
    llevels = channels.bit_length() - 1
    flevels = freq_count.bit_length() - 1
    blevels = flevels - split
    samples = chunks * LANES
    block = chunks // sets
    count = block // SUB
    lowest = freq_count // sets
    nwidth = w_ref.shape[0]
    xv, st_own, st_peer, pack, hpeer = (ref[n] for n in ("xv", "st_own", "st_peer", "pack", "hpeer"))
    fin, tri, scl = ref["fin"], ref["tri"], ref["scl"]

    tm = lax.axis_index("tm")
    freq = lax.axis_index("freq")
    k = freq // lowest
    f0 = freq % lowest
    peer = {"tm": 1 - tm}
    zs = [flip(k, m) for m in range(sets)]
    same = [{"freq": zs[m] * lowest + f0} for m in range(sets)]
    cross = [{"freq": zs[m] * lowest + f0, "tm": 1 - tm} for m in range(sets)]
    sides = [(freq // 2**j) % 2 for j in range(blevels)]
    partners = [{"freq": flip(freq, 2**j)} for j in range(blevels)]
    remote = [m for m in RAW_ORDER if m < sets] if sets > 1 else []

    barrier = pltpu.get_barrier_semaphore()
    others = [peer] + partners + [same[m] for m in remote] + [cross[m] for m in remote]
    for other in others:
        pl.semaphore_signal(barrier, inc=1, device_id=other, device_id_type=MESH)

    c0_of = [block - SUB * (p + 1) for p in range(count)]

    def rows_of(first, size):
        return pl.ds(pl.multiple_of(first * SUB, SUB), size * SUB)

    load_x = pltpu.make_async_copy(x_ref, xv, ref["lsem"].at[0])
    load_x.start()
    own_loads = []
    for p in range(count):
        own_loads.append(pltpu.make_async_copy(
            x_ref.at[:, rows_of(k * block + c0_of[p], SUB), :], ref["raw", 0, p], ref["osem"].at[p],
        ))
    own_halo = pltpu.make_async_copy(
        x_ref.at[:, rows_of(jnp.minimum((k + 1) * block, chunks - halo_chunks), halo_chunks), :],
        ref["rawh", 0], ref["lsem"].at[1],
    )
    for copy in own_loads + [own_halo]:
        copy.start()

    sent = []

    def push(src, dst, ssem, rsem, device):
        copy = pltpu.make_async_remote_copy(
            src_ref=src, dst_ref=dst, send_sem=ssem, recv_sem=rsem,
            device_id=device, device_id_type=MESH,
        )
        sent.append(copy)
        return copy

    peer_halo = push(
        x_ref.at[:, pl.ds(0, halo_chunks * SUB), :], hpeer,
        ref["psem"].at[0], ref["psem"].at[1], peer,
    )
    stat_copy = push(st_own, st_peer, ref["psem"].at[2], ref["psem"].at[3], peer)
    raw_copies, halo_copies, pack_copies, table_copies = {}, {}, {}, {}
    for m in remote:
        last = zs[m] == sets - 1
        halo_copies[m] = push(
            x_ref.at[:, rows_of(jnp.where(last, 0, (zs[m] + 1) * block), halo_chunks), :],
            ref["rawh", m], ref["hsend"].at[m], ref["hrecv"].at[m],
            {"freq": zs[m] * lowest + f0, "tm": jnp.where(last, 1 - tm, tm)},
        )
        for p in range(count):
            raw_copies[p, m] = push(
                x_ref.at[:, rows_of(zs[m] * block + c0_of[p], SUB), :], ref["raw", m, p],
                ref["rsend"].at[p, m], ref["rrecv"].at[p, m], same[m],
            )
        pack_copies[m] = push(
            pack, ref["pack", m], ref["ksend"].at[m], ref["krecv"].at[m], same[m],
        )
        table_copies[m] = [
            push(ld_ref, ref["ld", m], ref["tsend"].at[0, m], ref["trecv"].at[0, m], same[m]),
            push(md_ref, ref["md", m], ref["tsend"].at[1, m], ref["trecv"].at[1, m], same[m]),
        ]

    pl.semaphore_wait(barrier, len(others))
    for m in remote:
        halo_copies[m].start()
        raw_copies[0, m].start()
    peer_halo.start()

    lane = lax.broadcasted_iota(jnp.int32, (SUB, LANES), 1)
    load_x.wait()
    for g in range(groups):
        data = xv[g].reshape(chunks, SUB, LANES)
        mean = jnp.sum(jnp.sum(data, axis=0), axis=1, keepdims=True) / samples
        off = data - mean[None]
        square = jnp.sum(jnp.sum(off * off, axis=0), axis=1, keepdims=True)
        st_own[0, pl.ds(g * SUB, SUB), :] = jnp.broadcast_to(mean, (SUB, LANES))
        st_own[1, pl.ds(g * SUB, SUB), :] = jnp.broadcast_to(square, (SUB, LANES))
    stat_copy.start()
    for m in remote:
        for copy in table_copies[m]:
            copy.start()

    before = lax.broadcasted_iota(jnp.int32, (LANES, 2 * LANES), 0)
    after = lax.broadcasted_iota(jnp.int32, (LANES, 2 * LANES), 1)
    tri[...] = jnp.where(before < after, 1.0, 0.0)
    norm = 1.0 / math.sqrt(channels * freq_count)
    for i in range(nwidth):
        wide = jnp.full((SUB, LANES), w_ref[i].astype(jnp.float32), jnp.float32)
        scl[i] = (1.0 / jnp.sqrt(wide)) * norm

    stat_copy.wait_recv()
    mean_a, mean_b = st_own[0], st_peer[0]
    gap = mean_a - mean_b
    variance = (st_own[1] + st_peer[1] + gap * gap * (samples / 2)) / (2 * samples)
    mean_all = (mean_a + mean_b) * 0.5
    gain_all = 1.0 / jnp.sqrt(variance + EPSILON)
    ref["nrm", 0][0] = mean_all
    ref["nrm", 0][1] = gain_all
    wide = LANES // (2 * groups)
    packed = gain_all[(groups - 1) * SUB :]
    for g in reversed(range(groups)):
        if g < groups - 1:
            packed = jnp.where(lane < (2 * g + 2) * wide, gain_all[g * SUB : (g + 1) * SUB], packed)
        packed = jnp.where(lane < (2 * g + 1) * wide, mean_all[g * SUB : (g + 1) * SUB], packed)
    if remote:
        pack[...] = packed
    for m in remote:
        pack_copies[m].start()
    for p in range(1, count):
        for m in remote:
            raw_copies[p, m].start()

    keep = jnp.where((tm == 1) & (k == sets - 1), 0.0, 1.0)
    halo_size = -(-halo_chunks // SUB) * SUB

    def side_of(m, i):
        bit = (k // 2**i) % 2
        return 1 - bit if (m >> i) & 1 else bit

    def source(level, p, m):
        if level < blevels:
            return ref["bf", level, p, m], c0_of[p]
        i = level - blevels
        return ref["pb", i, m & ~(1 << i)], 0

    def put(level, p, m, r, c0, size, value):
        buf, first = source(level, p, m)
        side = sides[level] if level < blevels else side_of(m, level - blevels)
        buf[side, r, pl.ds(c0 - first, size), :] = value

    def rows(body):
        for g in range(groups):
            body(g)

    def tiles(p):
        found = [(c0_of[p], SUB, False)]
        if p == 0:
            found.insert(0, (block, halo_size, True))
        return found

    def normalise(p, m, c0, size, is_halo):
        nrm = ref["nrm", m]

        def body(g):
            out = []
            for i in range(SUB):
                r = g * SUB + i
                gain = nrm[1, pl.ds(r, 1), :]
                if is_halo:
                    part = ref["rawh", m][g, pl.ds(i, halo_chunks, stride=SUB), :]
                    if m == 0:
                        part = jnp.where(
                            k == sets - 1, hpeer[g, pl.ds(i, halo_chunks, stride=SUB), :], part,
                        )
                    gain = gain * keep
                else:
                    part = ref["raw", m, p][g, pl.ds(i, size, stride=SUB), :]
                out.append((part - nrm[0, pl.ds(r, 1), :]) * gain)
            for i in range(SUB):
                n = halo_chunks if is_halo else size
                ref["loc", 0, m][g * SUB + i, pl.ds(c0, n), :] = out[i]

        rows(body)

    def merged(low, high, lag, span, c0, size):
        if span < LANES:
            jump = 0
        else:
            jump = lag // LANES
            lag = lag % LANES
        cur = high(c0 + jump, size)
        nxt = high(c0 + jump + 1, size)
        lanes = lax.broadcasted_iota(jnp.int32, (size, LANES), 1)
        mixed = jnp.where(lanes < lag, nxt, cur)
        return low(c0, size) + pltpu.roll(mixed, (LANES - lag) % LANES, 1)

    def local_level(s, p, m, c0, size):
        span = 2**s
        src = ref["loc", s, m]
        table = ref["ld", m] if m else ld_ref

        def body(g):
            out = []
            for i in range(SUB):
                r = g * SUB + i
                base = (r // (2 * span)) * (2 * span)
                lo_row = base + table[0, s, r]
                hi_row = base + span + table[1, s, r]
                out.append(merged(
                    lambda c, n: src[lo_row, pl.ds(c, n), :],
                    lambda c, n: src[hi_row, pl.ds(c, n), :],
                    table[2, s, r], span, c0, size,
                ))
            for i in range(SUB):
                r = g * SUB + i
                if s + 1 < llevels:
                    ref["loc", s + 1, m][r, pl.ds(c0, size), :] = out[i]
                else:
                    put(0, p, m, r, c0, size, out[i])

        rows(body)

    def merge_level(j, p, m, c0, size):
        span = channels * 2**j
        src, first = source(j, p, m)
        table = ref["md", m] if m else md_ref

        def body(g):
            out = []
            for i in range(SUB):
                r = g * SUB + i
                lo_row = table[j, 0, r]
                hi_row = table[j, 1, r]
                out.append(merged(
                    lambda c, n: src[0, lo_row, pl.ds(c, n), :],
                    lambda c, n: src[1, hi_row, pl.ds(c, n), :],
                    table[j, 2, r], span, c0 - first, size,
                ))
            for i in range(SUB):
                r = g * SUB + i
                if j + 1 < flevels:
                    put(j + 1, p, m, r, c0, size, out[i])
                else:
                    fin[pl.ds(r * SUB, SUB), :] = out[i]

        rows(body)

    def prefix(m, c0):
        sums = jnp.dot(
            fin[...], tri[...], precision=lax.Precision.HIGHEST,
            preferred_element_type=jnp.float32,
        )
        own = sums[:, :LANES].reshape(channels, SUB, LANES)
        ref["eb", m][:, pl.ds(c0, SUB), :] = own
        return own, sums[:, LANES:].reshape(channels, SUB, LANES)

    def boxcar(p, m, c0):
        own, total = prefix(m, c0)
        far = total + ref["eb", m][:, pl.ds(c0 + 1, SUB), :]
        lanes = lax.broadcasted_iota(jnp.int32, (channels, SUB, LANES), 2)

        def body(at, best):
            for u in range(unroll):
                i = at * unroll + u
                wide = w_ref[i]
                mixed = jnp.where(lanes < wide, far, own)
                ahead = pltpu.roll(mixed, LANES - wide, 2)
                best = jnp.maximum(best, (ahead - own) * scl[i][None])
            return best

        unroll = math.gcd(nwidth, UNROLL)
        best = lax.fori_loop(
            0, nwidth // unroll, body, jnp.full((channels, SUB, LANES), -jnp.inf, jnp.float32)
        )
        for r in range(channels):
            g, i = r // SUB, r % SUB
            if m:
                ref["res", p, m][g, pl.ds(i, SUB, stride=SUB), :] = best[r]
            else:
                at = pl.multiple_of((k * block + c0) * SUB, SUB) + i
                o_ref[g, pl.ds(at, SUB, stride=SUB), :] = best[r]

    level_copies = {}
    for j in range(blevels):
        for p in range(count):
            for m in range(sets):
                size = SUB + (halo_chunks if p == 0 else 0)
                window = ref["bf", j, p, m].at[sides[j], :, pl.ds(0, size), :]
                level_copies[j, p, m] = push(
                    window, window, ref["bsend"].at[j, p, m], ref["brecv"].at[j, p, m], partners[j],
                )
    result_copies = {}
    for p in range(count):
        for m in remote:
            result_copies[p, m] = push(
                ref["res", p, m], o_ref.at[:, rows_of(k * block + c0_of[p], SUB), :],
                ref["osend"].at[p, m], ref["orecv"].at[p, m], same[m],
            )

    def local_stage(p, m):
        if m:
            if p == 0:
                for copy in [halo_copies[m], pack_copies[m]] + table_copies[m]:
                    copy.wait_recv()
                got = ref["pack", m][...]
                for g in range(groups):
                    for i in range(2):
                        at = (2 * g + i) * wide
                        ref["nrm", m][i, pl.ds(g * SUB, SUB), :] = jnp.broadcast_to(
                            got[:, at : at + 1], (SUB, LANES)
                        )
            raw_copies[p, m].wait_recv()
        else:
            if p == 0:
                own_halo.wait()
                peer_halo.wait_recv()
            own_loads[p].wait()
        for c0, size, is_halo in tiles(p):
            normalise(p, m, c0, size, is_halo)
            for s in range(llevels):
                local_level(s, p, m, c0, size)
        if blevels:
            level_copies[0, p, m].start()

    def merge_stage(j, p, m):
        if j < blevels:
            level_copies[j, p, m].wait_recv()
            if p:
                over = channels * 2**j // LANES + 1
                ref["bf", j, p, m][:, :, pl.ds(SUB, over), :] = ref["bf", j, p - 1, m][:, :, pl.ds(0, over), :]
        for c0, size, is_halo in tiles(p):
            if j + 1 < flevels:
                merge_level(j, p, m, c0, size)
            elif is_halo:
                merge_level(j, p, m, c0, SUB)
                prefix(m, c0)
            else:
                merge_level(j, p, m, c0, SUB)
                boxcar(p, m, c0)
        if j + 1 < blevels:
            level_copies[j + 1, p, m].start()
        if j + 1 == flevels and m:
            result_copies[p, m].start()

    if split == 0:
        lags = [FIRST_LAG] + [MID_LAG] * (flevels - 2) + [LAST_LAG]
        behind = [sum(lags[: j + 1]) for j in range(flevels)]
        for step in range(count + behind[-1]):
            if step < count:
                local_stage(step, 0)
            for j in range(flevels):
                if 0 <= step - behind[j] < count:
                    merge_stage(j, step - behind[j], 0)
    else:
        arrive = [m for m in LOCAL_ORDER if m < sets]
        leave = [m for m in LEAVE_ORDER if m < sets]
        local_stage(0, 0)
        local_stage(1, 0)
        for m in arrive:
            local_stage(0, m)
        for p in range(count):
            for j in range(flevels - 1):
                for m in [0] + arrive:
                    merge_stage(j, p, m)
            ready = list(arrive) if p + 1 < count else []
            for m in leave:
                merge_stage(flevels - 1, p, m)
                if ready:
                    local_stage(p + 1, ready.pop(0))
            for m in ready:
                local_stage(p + 1, m)
            if p + 2 < count:
                local_stage(p + 2, 0)
            merge_stage(flevels - 1, p, 0)

    for copy in result_copies.values():
        copy.wait_recv()
    for copy in sent:
        copy.wait_send()


RAW_ORDER = (3, 2, 1)
LOCAL_ORDER = (1, 3, 2)
LEAVE_ORDER = (3, 2, 1)


def per_device(mesh_shape, spectra, local_delays, merge_delays, widths):
    channels, block_len = spectra.shape
    freq_count = mesh_shape["freq"]
    chunks = block_len // LANES
    groups = channels // SUB
    halo_chunks = -(-(channels * freq_count - 1 + LANES) // LANES)
    llevels = channels.bit_length() - 1
    flevels = freq_count.bit_length() - 1
    split = 0
    while (
        split < min(MAX_SPLIT, flevels)
        and chunks % (SUB * 2 ** (split + 2)) == 0
        and 4 * halo_chunks <= chunks // 2 ** (split + 1)
    ):
        split += 1
    sets = 2**split
    block = chunks // sets
    count = block // SUB
    blevels = flevels - split
    halo_size = -(-halo_chunks // SUB) * SUB
    over = -(-(channels * freq_count // 2 // LANES + 1) // SUB) * SUB
    depth = block + halo_size + SUB
    f32 = jnp.float32
    flat = spectra.reshape(groups, SUB, chunks, LANES).transpose(0, 2, 1, 3)
    flat = flat.reshape(groups, chunks * SUB, LANES)
    dma = pltpu.SemaphoreType.DMA

    def vmem(*shape):
        return pltpu.VMEM(shape, f32)

    scratch = {
        "xv": vmem(*flat.shape),
        "st_own": vmem(2, channels, LANES),
        "st_peer": vmem(2, channels, LANES),
        "pack": vmem(SUB, LANES),
        "hpeer": vmem(groups, halo_chunks * SUB, LANES),
        "fin": vmem(channels * SUB, LANES),
        "tri": vmem(LANES, 2 * LANES),
        "scl": vmem(widths.shape[0], SUB, LANES),
        "lsem": dma((2,)),
        "osem": dma((count,)),
        "psem": dma((4,)),
        "hsend": dma((sets,)),
        "hrecv": dma((sets,)),
        "ksend": dma((sets,)),
        "krecv": dma((sets,)),
        "tsend": dma((2, sets)),
        "trecv": dma((2, sets)),
        "rsend": dma((count, sets)),
        "rrecv": dma((count, sets)),
        "osend": dma((count, sets)),
        "orecv": dma((count, sets)),
    }
    if blevels:
        scratch["bsend"] = dma((blevels, count, sets))
        scratch["brecv"] = dma((blevels, count, sets))
    for m in range(sets):
        scratch["rawh", m] = vmem(groups, halo_chunks * SUB, LANES)
        scratch["nrm", m] = vmem(2, channels, LANES)
        scratch["eb", m] = vmem(channels, depth, LANES)
        for s in range(llevels):
            scratch["loc", s, m] = vmem(channels, depth, LANES)
        for p in range(count):
            scratch["raw", m, p] = vmem(groups, SUB * SUB, LANES)
            tail = (halo_size if p == 0 else 0) + over
            for j in range(blevels):
                scratch["bf", j, p, m] = vmem(2, channels, SUB + tail, LANES)
            if m:
                scratch["res", p, m] = vmem(groups, SUB * SUB, LANES)
        for i in range(split):
            if not (m >> i) & 1:
                scratch["pb", i, m] = vmem(2, channels, block + halo_size + over, LANES)
        if m:
            scratch["pack", m] = vmem(SUB, LANES)
            scratch["ld", m] = pltpu.SMEM((3, llevels, channels), jnp.int32)
            scratch["md", m] = pltpu.SMEM((flevels, 3, channels), jnp.int32)

    smem = pl.BlockSpec(memory_space=pltpu.SMEM)
    geo = (channels, chunks, freq_count, halo_chunks, split)
    out = pl.pallas_call(
        functools.partial(kernel, geo, tuple(scratch)),
        out_shape=pltpu.VMEM(flat.shape, f32),
        in_specs=[pl.BlockSpec(memory_space=pl.ANY), smem, smem, smem],
        out_specs=pl.BlockSpec(memory_space=pltpu.VMEM),
        scratch_shapes=list(scratch.values()),
        compiler_params=pltpu.CompilerParams(
            collective_id=0, has_side_effects=True, vmem_limit_bytes=56 * 2**20
        ),
    )(flat, local_delays.transpose(1, 0, 2), merge_delays, widths)
    out = out.reshape(groups, chunks, SUB, LANES).transpose(0, 2, 1, 3)
    return out.reshape(channels, block_len)


def solution(mesh):
    placed = (P(("beam", "freq"), "tm"), P(None, None, "freq"), P(None, None, "freq"), P())
    return jax.shard_map(
        functools.partial(per_device, dict(mesh.shape)), mesh=mesh, in_specs=placed,
        out_specs=P(("beam", "freq"), "tm"), check_vma=False,
    )
```

time: 42.3 us -> 40.2 us (0.950)
  Pallas kernels: 41.4 us -> 39.2 us
    pallas_call x1, Pallas kernels: 41.4 us -> 39.2 us  [per_device(): pl.pallas_call(functools.partial(kernel, geo, tuple(scratch)), out_shape=...]
where the time goes in v1:
time: 40.2 us; the launch traced here: 40 us
  Pallas kernels  39.2 us (98%)
  local copies, waits for them, and re-layouts  0.8 us (2%)
    pallas_call x1, Pallas kernels, per_device(): pl.pallas_call(functools.partial(kernel, geo, tuple(scratch)), out_shape=...  39.2 us

profile of v1, /device:TPU:0, one launch (start us, length us, event | category | flops | bytes accessed | tf_op | source)
XLA Modules:
  0.0 40.0 jit_solution(1698752442899415175)
XLA Ops:
  0.0 39.2 %shard_map.46 = f32[2,512,128]{2,1,0:T(8,128)S(1)} custom-call(f32[2,512,128]{2,1,0:T(8,128)} %bitcast.12, s32[3,4,16]{2,1,0:T(4,128)} %bitcast.13, s32[3,3,16]{2,1,0:T(4,128)} %md_ref.1, s32[16]{0:T(128)} %w_ref.1), custom_call_target="tpu_custom_call" | custom-call | tf_op jit(solution)/shard_map/pallas_call | solution.py:503
  39.2 0.8 %copy.6 = f32[16,8192]{1,0:T(8,128)} copy(f32[16,8192]{1,0:T(8,128)S(1)} %bitcast.11) | data formatting | bytes 1048576

commit v2 on v1

--- a/solution.py
+++ b/solution.py
@@ -13,6 +13,15 @@
 LANES = 128
 SUB = 8
 MESH = pl.DeviceIdType.MESH
+RAW_ORDER = (3, 2, 1)
+LOCAL_ORDER = (1, 3, 2)
+LEAVE_ORDER = (2, 3, 1)
+DOWN_ORDER = (3, 2, 1)
+DOWN_FIRST = 1
+UP_ORDER = (1, 2, 3)
+INNER_AT = -1
+OUTER_AT = 2
+NEXT_AT = 1
 FIRST_LAG = 1
 MID_LAG = 1
 LAST_LAG = 3
@@ -58,9 +67,13 @@
     remote = [m for m in RAW_ORDER if m < sets] if sets > 1 else []
 
     barrier = pltpu.get_barrier_semaphore()
-    others = [peer] + partners + [same[m] for m in remote] + [cross[m] for m in remote]
-    for other in others:
+    for other in [peer] + partners:
         pl.semaphore_signal(barrier, inc=1, device_id=other, device_id_type=MESH)
+    for m in remote:
+        @pl.when(zs[m] > k)
+        def _(m=m):
+            for other in (same[m], cross[m]):
+                pl.semaphore_signal(barrier, inc=1, device_id=other, device_id_type=MESH)
 
     c0_of = [block - SUB * (p + 1) for p in range(count)]
 
@@ -117,11 +130,31 @@
             push(md_ref, ref["md", m], ref["tsend"].at[1, m], ref["trecv"].at[1, m], same[m]),
         ]
 
-    pl.semaphore_wait(barrier, len(others))
+    pl.semaphore_wait(barrier, 1 + blevels + (2 * k if remote else 0))
     for m in remote:
+        @pl.when(zs[m] < k)
+        def _(m=m):
+            for other in (same[m], cross[m]):
+                pl.semaphore_signal(ref["ready"].at[m], inc=1, device_id=other, device_id_type=MESH)
+    peer_halo.start()
+
+    def start_tables(m):
+        for copy in table_copies[m]:
+            copy.start()
+
+    def start_first(m):
         halo_copies[m].start()
         raw_copies[0, m].start()
-    peer_halo.start()
+
+    def at_distance(step, body):
+        for m in remote:
+            pl.when(zs[m] == k + step)(functools.partial(body, m))
+
+    for step in DOWN_ORDER:
+        at_distance(-step, start_tables)
+    for step in DOWN_ORDER[:DOWN_FIRST]:
+        at_distance(-step, start_first)
+    outer = (k == 0) | (k == sets - 1)
 
     lane = lax.broadcasted_iota(jnp.int32, (SUB, LANES), 1)
     load_x.wait()
@@ -133,9 +166,6 @@
         st_own[0, pl.ds(g * SUB, SUB), :] = jnp.broadcast_to(mean, (SUB, LANES))
         st_own[1, pl.ds(g * SUB, SUB), :] = jnp.broadcast_to(square, (SUB, LANES))
     stat_copy.start()
-    for m in remote:
-        for copy in table_copies[m]:
-            copy.start()
 
     before = lax.broadcasted_iota(jnp.int32, (LANES, 2 * LANES), 0)
     after = lax.broadcasted_iota(jnp.int32, (LANES, 2 * LANES), 1)
@@ -161,11 +191,27 @@
         packed = jnp.where(lane < (2 * g + 1) * wide, mean_all[g * SUB : (g + 1) * SUB], packed)
     if remote:
         pack[...] = packed
-    for m in remote:
+    for step in DOWN_ORDER:
+        at_distance(-step, lambda m: pack_copies[m].start())
+    for step in DOWN_ORDER[DOWN_FIRST:]:
+        at_distance(-step, start_first)
+
+    def start_up(m):
+        pl.semaphore_wait(ref["ready"].at[m], 2)
+        start_tables(m)
         pack_copies[m].start()
-    for p in range(1, count):
-        for m in remote:
-            raw_copies[p, m].start()
+        start_first(m)
+
+    for step in UP_ORDER:
+        at_distance(step, start_up)
+
+    def start_raw():
+        for p in range(1, count):
+            for m in remote:
+                raw_copies[p, m].start()
+
+    if remote and INNER_AT < 0:
+        pl.when(jnp.logical_not(outer))(start_raw)
 
     keep = jnp.where((tm == 1) & (k == sets - 1), 0.0, 1.0)
     halo_size = -(-halo_chunks // SUB) * SUB
@@ -393,19 +439,21 @@
         leave = [m for m in LEAVE_ORDER if m < sets]
         local_stage(0, 0)
         local_stage(1, 0)
-        for m in arrive:
+        for i, m in enumerate(arrive):
             local_stage(0, m)
+            if i == INNER_AT:
+                pl.when(jnp.logical_not(outer))(start_raw)
+            if i == OUTER_AT:
+                pl.when(outer)(start_raw)
         for p in range(count):
             for j in range(flevels - 1):
                 for m in [0] + arrive:
                     merge_stage(j, p, m)
-            ready = list(arrive) if p + 1 < count else []
-            for m in leave:
+            for i, m in enumerate(leave):
+                if i == NEXT_AT and p + 1 < count:
+                    for n in arrive:
+                        local_stage(p + 1, n)
                 merge_stage(flevels - 1, p, m)
-                if ready:
-                    local_stage(p + 1, ready.pop(0))
-            for m in ready:
-                local_stage(p + 1, m)
             if p + 2 < count:
                 local_stage(p + 2, 0)
             merge_stage(flevels - 1, p, 0)
@@ -414,11 +462,8 @@
         copy.wait_recv()
     for copy in sent:
         copy.wait_send()
-
-
-RAW_ORDER = (3, 2, 1)
 LOCAL_ORDER = (1, 3, 2)
-LEAVE_ORDER = (3, 2, 1)
+LEAVE_ORDER = (2, 3, 1)
 
 
 def per_device(mesh_shape, spectra, local_delays, merge_delays, widths):
@@ -473,6 +518,7 @@
         "rrecv": dma((count, sets)),
         "osend": dma((count, sets)),
         "orecv": dma((count, sets)),
+        "ready": pltpu.SemaphoreType.REGULAR((sets,)),
     }
     if blevels:
         scratch["bsend"] = dma((blevels, count, sets))

time: 40.2 us -> 36.9 us (0.918)
  Pallas kernels: 39.2 us -> 35.9 us
    pallas_call x1, Pallas kernels: 39.2 us -> 35.9 us  [per_device(): pl.pallas_call(functools.partial(kernel, geo, tuple(scratch)), out_shape=...]
where the time goes in v2:
time: 36.9 us; the launch traced here: 36.7 us
  Pallas kernels  35.9 us (97%)
  local copies, waits for them, and re-layouts  0.8 us (2%)
    pallas_call x1, Pallas kernels, per_device(): pl.pallas_call(functools.partial(kernel, geo, tuple(scratch)), out_shape=...  35.9 us
    unnamed x1, local copies, waits for them, and re-layouts  0.8 us

profile of v2, /device:TPU:0, one launch (start us, length us, event | category | flops | bytes accessed | tf_op | source)
XLA Modules:
  0.0 36.7 jit_solution(15791798524591486785)
XLA Ops:
  0.0 35.9 %shard_map.46 = f32[2,512,128]{2,1,0:T(8,128)S(1)} custom-call(f32[2,512,128]{2,1,0:T(8,128)} %bitcast.12, s32[3,4,16]{2,1,0:T(4,128)} %bitcast.13, s32[3,3,16]{2,1,0:T(4,128)} %md_ref.1, s32[16]{0:T(128)} %w_ref.1), custom_call_target="tpu_custom_call" | custom-call | tf_op jit(solution)/shard_map/pallas_call | solution.py:549
  35.9 0.8 %copy.6 = f32[16,8192]{1,0:T(8,128)} copy(f32[16,8192]{1,0:T(8,128)S(1)} %bitcast.11) | data formatting | bytes 1048576

commit v3 on v2

--- a/solution.py
+++ b/solution.py
@@ -17,7 +17,7 @@
 LOCAL_ORDER = (1, 3, 2)
 LEAVE_ORDER = (2, 3, 1)
 DOWN_ORDER = (3, 2, 1)
-DOWN_FIRST = 1
+DOWN_FIRST = 3
 UP_ORDER = (1, 2, 3)
 INNER_AT = -1
 OUTER_AT = 2
@@ -446,25 +446,33 @@
             if i == OUTER_AT:
                 pl.when(outer)(start_raw)
         for p in range(count):
-            for j in range(flevels - 1):
+            for j in range(blevels):
                 for m in [0] + arrive:
                     merge_stage(j, p, m)
+            built = set()
+
+            def build(j, m):
+                if (j, m) in built or j < blevels:
+                    return
+                built.add((j, m))
+                if j > blevels:
+                    build(j - 1, m & ~(1 << (j - blevels)))
+                    build(j - 1, m | (1 << (j - blevels)))
+                merge_stage(j, p, m)
+
             for i, m in enumerate(leave):
                 if i == NEXT_AT and p + 1 < count:
                     for n in arrive:
                         local_stage(p + 1, n)
-                merge_stage(flevels - 1, p, m)
+                build(flevels - 1, m)
             if p + 2 < count:
                 local_stage(p + 2, 0)
-            merge_stage(flevels - 1, p, 0)
+            build(flevels - 1, 0)
 
     for copy in result_copies.values():
         copy.wait_recv()
     for copy in sent:
         copy.wait_send()
-LOCAL_ORDER = (1, 3, 2)
-LEAVE_ORDER = (2, 3, 1)
-
 
 def per_device(mesh_shape, spectra, local_delays, merge_delays, widths):
     channels, block_len = spectra.shape

time: 36.9 us -> 36.5 us (0.989)
  no operation moved by 1% of the time
where the time goes in v3:
time: 36.5 us; the launch traced here: 36.4 us
  Pallas kernels  35.6 us (98%)
  local copies, waits for them, and re-layouts  0.8 us (2%)
    pallas_call x1, Pallas kernels, per_device(): pl.pallas_call(functools.partial(kernel, geo, tuple(scratch)), out_shape=...  35.6 us
    unnamed x1, local copies, waits for them, and re-layouts  0.8 us

profile of v3, /device:TPU:0, one launch (start us, length us, event | category | flops | bytes accessed | tf_op | source)
XLA Modules:
  0.0 36.4 jit_solution(9836370514885415300)
XLA Ops:
  0.0 35.6 %shard_map.46 = f32[2,512,128]{2,1,0:T(8,128)S(1)} custom-call(f32[2,512,128]{2,1,0:T(8,128)} %bitcast.12, s32[3,4,16]{2,1,0:T(4,128)} %bitcast.13, s32[3,3,16]{2,1,0:T(4,128)} %md_ref.1, s32[16]{0:T(128)} %w_ref.1), custom_call_target="tpu_custom_call" | custom-call | tf_op jit(solution)/shard_map/pallas_call | solution.py:557
  35.6 0.8 %copy.6 = f32[16,8192]{1,0:T(8,128)} copy(f32[16,8192]{1,0:T(8,128)S(1)} %bitcast.11) | data formatting | bytes 1048576
